TPU v7x, 32 devices: a whole 2x2x4 slice. The times are simulated.
32 devices in a mesh: gx: 4 (over y, x), gy: 8 (over z, core).
Axes of the slice: x: 2, y: 2, z: 4, core: 2. Of those that a mesh axis runs over, the one named last changes fastest.
Arguments:
- probes: float32 [24, 48, 64, 128], P('gx', 'gy'), may hold values from -6 to 6
- pair_blocks: float32 [24, 48, 9, 128, 128], P('gx', 'gy'), may hold values from -0.09375 to 0.09375
- partners: int32 [24, 48, 9], P('gx', 'gy'), may hold values from 0 to 1151, as said below
- shifts: int32 [2, 24, 48, 9], P(None, 'gx', 'gy'), may hold values from -1 to 1, as said below
- counts: int32 [24, 48], P('gx', 'gy'), may hold values from 1 to 9, as said below
- kpoint: float32 [2], replicated, may hold values from -3.140625 to 3.140625
Outputs:
- last_vector: float32 [24, 48, 64, 128], P('gx', 'gy')
- intersections: float32 [3, 2, 32], replicated
Inputs may be any that keep to these rules, and one draw needn't show every extreme that they name: `partners`: slot 0 of cell (x, y) names the cell itself; slots 1 to 8 name its eight neighbouring cells (x + dx, y + dy) with dx, dy in -1..1 taken periodically modulo 24 and 48, each once, in no fixed order. shifts[0, x, y, s] = (x + dx - px) / 24 and shifts[1, x, y, s] = (y + dy - py) / 48 for the slot's offset (dx, dy) and partner cell (px, py). `counts`: slots at or beyond a cell's count are padding; some cell has all 9 slots live.
All inputs are finite; a program needn't handle non-finite values.
Results may differ from a plain program's by a relative error of at most 0.0001.
Values sent between devices are 32-bit elements; how exact they have to be, the bound alone decides.
A program may use at most 128 MiB of HBM per device.

v0:
```python
import math
import jax
import jax.numpy as jnp
from jax import lax
from jax.sharding import PartitionSpec as P

STEPS = 3


def with_halo(cells, sides, width):
    for axis, dim in sides:
        count = lax.axis_size(axis)
        head = lax.slice_in_dim(cells, 0, width, axis=dim)
        tail = lax.slice_in_dim(cells, cells.shape[dim] - width, cells.shape[dim], axis=dim)
        cells = jnp.concatenate(
            [
                lax.ppermute(tail, axis, [(i, (i + 1) % count) for i in range(count)]),
                cells,
                lax.ppermute(head, axis, [((i + 1) % count, i) for i in range(count)]),
            ],
            axis=dim,
        )
    return cells


def intersection(first, other):
    half = first.shape[2] // 2
    first_re, first_im = (first[:, :, :half], first[:, :, half:])
    other_re, other_im = (other[:, :, :half], other[:, :, half:])
    real_part = jnp.sum(first_re * other_re + first_im * other_im, axis=(0, 1, 3))
    imag_part = jnp.sum(first_re * other_im - first_im * other_re, axis=(0, 1, 3))
    return jnp.stack([real_part, imag_part])


def extend(field):
    return with_halo(field, (("gx", 0), ("gy", 1)), 1)


def shards(probes, pair_blocks, partners, shifts, counts, kpoint):
    cells_x, cells_y, width, block = probes.shape
    slot_total = pair_blocks.shape[2]
    half = width // 2
    cells = cells_x * cells_y
    total_x = cells_x * lax.axis_size("gx")
    total_y = cells_y * lax.axis_size("gy")
    start_x = lax.axis_index("gx") * cells_x
    start_y = lax.axis_index("gy") * cells_y
    partner_x = partners // total_y
    partner_y = partners % total_y
    local_x = jnp.mod(partner_x - start_x + 1, total_x)
    local_y = jnp.mod(partner_y - start_y + 1, total_y)
    flat_partner = (local_x * (cells_y + 2) + local_y).reshape(cells, slot_total)
    angle = kpoint[0] * shifts[0].astype(jnp.float32) + kpoint[1] * shifts[1].astype(jnp.float32)
    angle = angle.reshape(cells, slot_total)
    live = (jnp.arange(slot_total, dtype=jnp.int32)[None, :] < counts.reshape(cells, 1)).astype(
        jnp.float32
    )
    cosine = jnp.cos(angle) * live
    sine = jnp.sin(angle) * live
    blocks = pair_blocks.reshape(cells, slot_total, block, block)
    slot_bound = jnp.max(counts)

    def apply_hamiltonian(field):
        source = extend(field).reshape(-1, width, block)

        def accumulate(slot, sums):
            real_sum, imag_sum = sums
            piece = jnp.take(source, flat_partner[:, slot], axis=0)
            chosen = lax.dynamic_index_in_dim(blocks, slot, 1, keepdims=False)
            product = jnp.einsum("npb,nba->npa", piece, chosen, precision=lax.Precision.HIGHEST)
            cos_part = lax.dynamic_index_in_dim(cosine, slot, 1, keepdims=False)[:, None, None]
            sin_part = lax.dynamic_index_in_dim(sine, slot, 1, keepdims=False)[:, None, None]
            real_part = product[:, :half]
            imag_part = product[:, half:]
            return (
                real_sum + cos_part * real_part - sin_part * imag_part,
                imag_sum + sin_part * real_part + cos_part * imag_part,
            )

        zeros = jnp.zeros((cells, half, block), jnp.float32)
        real_sum, imag_sum = lax.fori_loop(0, slot_bound, accumulate, (zeros, zeros))
        return jnp.concatenate([real_sum, imag_sum], axis=1).reshape(field.shape)

    scale = 1.0 / math.sqrt(total_x * total_y * block)

    def reduce_one(field):
        return lax.psum(intersection(probes, field), ("gx", "gy")) * scale

    before = probes
    current = apply_hamiltonian(probes)
    partial_list = []
    partial_list.append(reduce_one(current))
    for step in range(STEPS - 1):
        following = 2.0 * apply_hamiltonian(current) - before
        before, current = (current, following)
        partial_list.append(reduce_one(current))
    found = jnp.stack(partial_list)
    return (current, found)


def solution(mesh):
    placed = (
        P("gx", "gy", None, None),
        P("gx", "gy", None, None, None),
        P("gx", "gy", None),
        P(None, "gx", "gy", None),
        P("gx", "gy"),
        P(),
    )
    return jax.shard_map(
        shards,
        mesh=mesh,
        in_specs=placed,
        out_specs=(P("gx", "gy", None, None), P()),
        check_vma=False,
    )
```

profile of v0, /device:TPU:0, one launch (start us, length us, event | category | flops | bytes accessed | tf_op | source)
XLA Modules:
  0.0 336.3 jit_solution(18082595083658992762)
XLA Ops:
  0.6 1.1 fusion.46
  1.8 3.0 collective-permute-start
  4.8 1.0 collective-permute-start.1
  5.8 1.3 fusion.47
  7.1 2.8 sine_reduce_fusion
  11.6 3.5 %collective-permute-done.1 = f32[1,6,64,128]{3,2,1,0:T(8,128)S(1)} collective-permute-done((f32[1,6,64,128]{3,2,1,0:T(8,128)S(1)}, f32[1,6,64,128]{3,2,1,0:T(8,128)S(1)}, u32[]{:S(2)}, u32[]{:S(2)}) %collective-permute-start.1) | collective-permute-done | bytes 196640 | tf_op jit(solution)/shard_map/ppermute | solution.py:19
  15.2 1.2 copy-done.21
  16.5 3.5 %collective-permute-start.3 = (f32[8,1,64,128]{3,2,1,0:T(8,128)S(1)}, f32[8,1,64,128]{3,2,1,0:T(8,128)S(1)}, u32[]{:S(2)}, u32[]{:S(2)}) collective-permute-start(f32[8,1,64,128]{3,2,1,0:T(8,128)S(1)} %get-tuple-element.273), channel_id=1, source_target_pairs={{1,0},{2,1},{3,2},{4,3},{5,4},{6,5},{7,6},{0,7},{9,8},{10,9},{11,1... | collective-permute-start | bytes 786440 | tf_op jit(solution)/shard_map/ppermute | solution.py:19
  20.4 15.5 %copy.12 = f32[6,6,9,128,128]{4,3,1,0,2:T(8,128)} copy(f32[6,6,9,128,128]{4,3,2,1,0:T(8,128)} %param.15) | data formatting | bytes 42467328 | tf_op args[1]
  36.5 1.6 pad_maximum_fusion
  38.1 0.9 broadcast.33.clone.3
  39.0 0.9 broadcast.33.clone.4
  39.9 67.6 %while.36 = (s32[]{:T(128)}, f32[36,32,128]{2,1,0:T(8,128)}, f32[36,32,128]{2,1,0:T(8,128)}, s32[]{:T(128)}, f32[36,9]{0,1:T(8,128)S(1)}, /*index=5*/s32[36,9]{0...) while((s32[]{:T(128)}, f32[36,32,128]{2,1,0:T(8,128)}, ...), condition=%wide.region_2.4_spmd, body=%wide.region_1.3_spmd.sunk | while | flops 454460640 | bytes 20059900 | solution.py:81
  41.2 4.0 %fusion.62 = f32[36,64,128]{2,1,0:T(8,128)S(1)} fusion(f32[36,9,128,128]{3,2,0,1:T(8,128)} %get-tuple-element.523, s32[]{:T(128)S(6)} %select_n.106, f32[36,64,128]{2,1,0:T(8,128)S(1)} %gather_fusion, pred[36]{0:T(512)(128)(4,1)S(1)} %get-tuple-element.457), kind=kOutput, calls=%fused_computation.3.clone.1 | convolution fusion | flops 453279744 | bytes 4718632 | tf_op jit(solution)/shard_map/while/body/npb,nba->npa/dot_general | solution.py:70
  48.7 4.0 %fusion.62 = f32[36,64,128]{2,1,0:T(8,128)S(1)} fusion(f32[36,9,128,128]{3,2,0,1:T(8,128)} %get-tuple-element.523, s32[]{:T(128)S(6)} %select_n.106, f32[36,64,128]{2,1,0:T(8,128)S(1)} %gather_fusion, pred[36]{0:T(512)(128)(4,1)S(1)} %get-tuple-element.457), kind=kOutput, calls=%fused_computation.3.clone.1 | convolution fusion | flops 453279744 | bytes 4718632 | tf_op jit(solution)/shard_map/while/body/npb,nba->npa/dot_general | solution.py:70
  56.1 4.0 %fusion.62 = f32[36,64,128]{2,1,0:T(8,128)S(1)} fusion(f32[36,9,128,128]{3,2,0,1:T(8,128)} %get-tuple-element.523, s32[]{:T(128)S(6)} %select_n.106, f32[36,64,128]{2,1,0:T(8,128)S(1)} %gather_fusion, pred[36]{0:T(512)(128)(4,1)S(1)} %get-tuple-element.457), kind=kOutput, calls=%fused_computation.3.clone.1 | convolution fusion | flops 453279744 | bytes 4718632 | tf_op jit(solution)/shard_map/while/body/npb,nba->npa/dot_general | solution.py:70
  63.5 4.0 %fusion.62 = f32[36,64,128]{2,1,0:T(8,128)S(1)} fusion(f32[36,9,128,128]{3,2,0,1:T(8,128)} %get-tuple-element.523, s32[]{:T(128)S(6)} %select_n.106, f32[36,64,128]{2,1,0:T(8,128)S(1)} %gather_fusion, pred[36]{0:T(512)(128)(4,1)S(1)} %get-tuple-element.457), kind=kOutput, calls=%fused_computation.3.clone.1 | convolution fusion | flops 453279744 | bytes 4718632 | tf_op jit(solution)/shard_map/while/body/npb,nba->npa/dot_general | solution.py:70
  71.0 4.0 %fusion.62 = f32[36,64,128]{2,1,0:T(8,128)S(1)} fusion(f32[36,9,128,128]{3,2,0,1:T(8,128)} %get-tuple-element.523, s32[]{:T(128)S(6)} %select_n.106, f32[36,64,128]{2,1,0:T(8,128)S(1)} %gather_fusion, pred[36]{0:T(512)(128)(4,1)S(1)} %get-tuple-element.457), kind=kOutput, calls=%fused_computation.3.clone.1 | convolution fusion | flops 453279744 | bytes 4718632 | tf_op jit(solution)/shard_map/while/body/npb,nba->npa/dot_general | solution.py:70
  78.4 4.0 %fusion.62 = f32[36,64,128]{2,1,0:T(8,128)S(1)} fusion(f32[36,9,128,128]{3,2,0,1:T(8,128)} %get-tuple-element.523, s32[]{:T(128)S(6)} %select_n.106, f32[36,64,128]{2,1,0:T(8,128)S(1)} %gather_fusion, pred[36]{0:T(512)(128)(4,1)S(1)} %get-tuple-element.457), kind=kOutput, calls=%fused_computation.3.clone.1 | convolution fusion | flops 453279744 | bytes 4718632 | tf_op jit(solution)/shard_map/while/body/npb,nba->npa/dot_general | solution.py:70
  85.9 4.0 %fusion.62 = f32[36,64,128]{2,1,0:T(8,128)S(1)} fusion(f32[36,9,128,128]{3,2,0,1:T(8,128)} %get-tuple-element.523, s32[]{:T(128)S(6)} %select_n.106, f32[36,64,128]{2,1,0:T(8,128)S(1)} %gather_fusion, pred[36]{0:T(512)(128)(4,1)S(1)} %get-tuple-element.457), kind=kOutput, calls=%fused_computation.3.clone.1 | convolution fusion | flops 453279744 | bytes 4718632 | tf_op jit(solution)/shard_map/while/body/npb,nba->npa/dot_general | solution.py:70
  93.3 4.0 %fusion.62 = f32[36,64,128]{2,1,0:T(8,128)S(1)} fusion(f32[36,9,128,128]{3,2,0,1:T(8,128)} %get-tuple-element.523, s32[]{:T(128)S(6)} %select_n.106, f32[36,64,128]{2,1,0:T(8,128)S(1)} %gather_fusion, pred[36]{0:T(512)(128)(4,1)S(1)} %get-tuple-element.457), kind=kOutput, calls=%fused_computation.3.clone.1 | convolution fusion | flops 453279744 | bytes 4718632 | tf_op jit(solution)/shard_map/while/body/npb,nba->npa/dot_general | solution.py:70
  100.7 4.0 %fusion.62 = f32[36,64,128]{2,1,0:T(8,128)S(1)} fusion(f32[36,9,128,128]{3,2,0,1:T(8,128)} %get-tuple-element.523, s32[]{:T(128)S(6)} %select_n.106, f32[36,64,128]{2,1,0:T(8,128)S(1)} %gather_fusion, pred[36]{0:T(512)(128)(4,1)S(1)} %get-tuple-element.457), kind=kOutput, calls=%fused_computation.3.clone.1 | convolution fusion | flops 453279744 | bytes 4718632 | tf_op jit(solution)/shard_map/while/body/npb,nba->npa/dot_general | solution.py:70
  107.5 1.2 constant_dynamic-update-slice_fusion.4
  108.8 1.5 collective-permute-start.4
  110.4 1.4 collective-permute-start.5
  111.8 5.0 %collective-permute-done.4 = f32[1,6,64,128]{3,2,1,0:T(8,128)S(1)} collective-permute-done((f32[1,6,64,128]{3,2,1,0:T(8,128)S(1)}, f32[1,6,64,128]{3,2,1,0:T(8,128)S(1)}, u32[]{:S(2)}, u32[]{:S(2)}) %collective-permute-start.4) | collective-permute-done | bytes 196640 | tf_op jit(solution)/shard_map/ppermute | solution.py:17
  116.8 1.0 collective-permute-done.5
  118.6 3.5 %collective-permute-start.7 = (f32[8,1,64,128]{3,2,1,0:T(8,128)S(1)}, f32[8,1,64,128]{3,2,1,0:T(8,128)}, u32[]{:S(2)}, u32[]{:S(2)}) collective-permute-start(f32[8,1,64,128]{3,2,1,0:T(8,128)S(1)} %get-tuple-element.271), channel_id=1, source_target_pairs={{1,0},{2,1},{3,2},{4,3},{5,4},{6,5},{7,6},{0,7},{9,8},{10,9},{11,1... | collective-permute-start | bytes 786440 | tf_op jit(solution)/shard_map/ppermute | solution.py:19
  122.1 5.8 %collective-permute-done.6 = f32[8,1,64,128]{3,2,1,0:T(8,128)S(1)} collective-permute-done((f32[8,1,64,128]{3,2,1,0:T(8,128)S(1)}, f32[8,1,64,128]{3,2,1,0:T(8,128)S(1)}, u32[]{:S(2)}, u32[]{:S(2)}) %collective-permute-start.6) | collective-permute-done | bytes 262176 | tf_op jit(solution)/shard_map/ppermute | solution.py:17
  128.6 1.3 pad_maximum_fusion.1
  130.0 0.9 broadcast.33.clone.1
  130.9 0.9 broadcast.33.clone.2
  131.7 67.6 %while.37 = (s32[]{:T(128)}, f32[36,32,128]{2,1,0:T(8,128)}, f32[36,32,128]{2,1,0:T(8,128)}, s32[]{:T(128)}, f32[36,9]{0,1:T(8,128)S(1)}, /*index=5*/s32[36,9]{0...) while((s32[]{:T(128)}, f32[36,32,128]{2,1,0:T(8,128)}, ...), condition=%wide.region_4.6_spmd, body=%wide.region_3.5_spmd.sunk | while | flops 454460640 | bytes 20059900 | solution.py:81
  133.1 4.0 %fusion.66 = f32[36,64,128]{2,1,0:T(8,128)S(1)} fusion(f32[36,9,128,128]{3,2,0,1:T(8,128)} %get-tuple-element.559, s32[]{:T(128)S(6)} %select_n.108, f32[36,64,128]{2,1,0:T(8,128)S(1)} %gather_fusion.1, pred[36]{0:T(512)(128)(4,1)S(1)} %get-tuple-element.472), kind=kOutput, calls=%fused_computation.22.clone.1 | convolution fusion | flops 453279744 | bytes 4718632 | tf_op jit(solution)/shard_map/while/body/npb,nba->npa/dot_general | solution.py:70
  140.5 4.0 %fusion.66 = f32[36,64,128]{2,1,0:T(8,128)S(1)} fusion(f32[36,9,128,128]{3,2,0,1:T(8,128)} %get-tuple-element.559, s32[]{:T(128)S(6)} %select_n.108, f32[36,64,128]{2,1,0:T(8,128)S(1)} %gather_fusion.1, pred[36]{0:T(512)(128)(4,1)S(1)} %get-tuple-element.472), kind=kOutput, calls=%fused_computation.22.clone.1 | convolution fusion | flops 453279744 | bytes 4718632 | tf_op jit(solution)/shard_map/while/body/npb,nba->npa/dot_general | solution.py:70
  148.0 4.0 %fusion.66 = f32[36,64,128]{2,1,0:T(8,128)S(1)} fusion(f32[36,9,128,128]{3,2,0,1:T(8,128)} %get-tuple-element.559, s32[]{:T(128)S(6)} %select_n.108, f32[36,64,128]{2,1,0:T(8,128)S(1)} %gather_fusion.1, pred[36]{0:T(512)(128)(4,1)S(1)} %get-tuple-element.472), kind=kOutput, calls=%fused_computation.22.clone.1 | convolution fusion | flops 453279744 | bytes 4718632 | tf_op jit(solution)/shard_map/while/body/npb,nba->npa/dot_general | solution.py:70
  155.4 4.0 %fusion.66 = f32[36,64,128]{2,1,0:T(8,128)S(1)} fusion(f32[36,9,128,128]{3,2,0,1:T(8,128)} %get-tuple-element.559, s32[]{:T(128)S(6)} %select_n.108, f32[36,64,128]{2,1,0:T(8,128)S(1)} %gather_fusion.1, pred[36]{0:T(512)(128)(4,1)S(1)} %get-tuple-element.472), kind=kOutput, calls=%fused_computation.22.clone.1 | convolution fusion | flops 453279744 | bytes 4718632 | tf_op jit(solution)/shard_map/while/body/npb,nba->npa/dot_general | solution.py:70
  162.8 4.0 %fusion.66 = f32[36,64,128]{2,1,0:T(8,128)S(1)} fusion(f32[36,9,128,128]{3,2,0,1:T(8,128)} %get-tuple-element.559, s32[]{:T(128)S(6)} %select_n.108, f32[36,64,128]{2,1,0:T(8,128)S(1)} %gather_fusion.1, pred[36]{0:T(512)(128)(4,1)S(1)} %get-tuple-element.472), kind=kOutput, calls=%fused_computation.22.clone.1 | convolution fusion | flops 453279744 | bytes 4718632 | tf_op jit(solution)/shard_map/while/body/npb,nba->npa/dot_general | solution.py:70
  170.3 4.0 %fusion.66 = f32[36,64,128]{2,1,0:T(8,128)S(1)} fusion(f32[36,9,128,128]{3,2,0,1:T(8,128)} %get-tuple-element.559, s32[]{:T(128)S(6)} %select_n.108, f32[36,64,128]{2,1,0:T(8,128)S(1)} %gather_fusion.1, pred[36]{0:T(512)(128)(4,1)S(1)} %get-tuple-element.472), kind=kOutput, calls=%fused_computation.22.clone.1 | convolution fusion | flops 453279744 | bytes 4718632 | tf_op jit(solution)/shard_map/while/body/npb,nba->npa/dot_general | solution.py:70
  177.7 4.0 %fusion.66 = f32[36,64,128]{2,1,0:T(8,128)S(1)} fusion(f32[36,9,128,128]{3,2,0,1:T(8,128)} %get-tuple-element.559, s32[]{:T(128)S(6)} %select_n.108, f32[36,64,128]{2,1,0:T(8,128)S(1)} %gather_fusion.1, pred[36]{0:T(512)(128)(4,1)S(1)} %get-tuple-element.472), kind=kOutput, calls=%fused_computation.22.clone.1 | convolution fusion | flops 453279744 | bytes 4718632 | tf_op jit(solution)/shard_map/while/body/npb,nba->npa/dot_general | solution.py:70
  185.2 4.0 %fusion.66 = f32[36,64,128]{2,1,0:T(8,128)S(1)} fusion(f32[36,9,128,128]{3,2,0,1:T(8,128)} %get-tuple-element.559, s32[]{:T(128)S(6)} %select_n.108, f32[36,64,128]{2,1,0:T(8,128)S(1)} %gather_fusion.1, pred[36]{0:T(512)(128)(4,1)S(1)} %get-tuple-element.472), kind=kOutput, calls=%fused_computation.22.clone.1 | convolution fusion | flops 453279744 | bytes 4718632 | tf_op jit(solution)/shard_map/while/body/npb,nba->npa/dot_general | solution.py:70
  192.6 4.0 %fusion.66 = f32[36,64,128]{2,1,0:T(8,128)S(1)} fusion(f32[36,9,128,128]{3,2,0,1:T(8,128)} %get-tuple-element.559, s32[]{:T(128)S(6)} %select_n.108, f32[36,64,128]{2,1,0:T(8,128)S(1)} %gather_fusion.1, pred[36]{0:T(512)(128)(4,1)S(1)} %get-tuple-element.472), kind=kOutput, calls=%fused_computation.22.clone.1 | convolution fusion | flops 453279744 | bytes 4718632 | tf_op jit(solution)/shard_map/while/body/npb,nba->npa/dot_general | solution.py:70
  199.4 1.4 maximum_multiply_fusion
  201.3 2.9 collective-permute-start.9
  204.2 5.7 %collective-permute-done.8 = f32[1,6,64,128]{3,2,1,0:T(8,128)S(1)} collective-permute-done((f32[1,6,64,128]{3,2,1,0:T(8,128)S(1)}, f32[1,6,64,128]{3,2,1,0:T(8,128)S(1)}, u32[]{:S(2)}, u32[]{:S(2)}) %collective-permute-start.8) | collective-permute-done | bytes 196640 | tf_op jit(solution)/shard_map/ppermute | solution.py:17
  211.3 3.5 %collective-permute-start.11 = (f32[8,1,64,128]{3,2,1,0:T(8,128)S(1)}, f32[8,1,64,128]{3,2,1,0:T(8,128)}, u32[]{:S(2)}, u32[]{:S(2)}) collective-permute-start(f32[8,1,64,128]{3,2,1,0:T(8,128)S(1)} %get-tuple-element.269), channel_id=1, source_target_pairs={{1,0},{2,1},{3,2},{4,3},{5,4},{6,5},{7,6},{0,7},{9,8},{10,9},{11,1... | collective-permute-start | bytes 786440 | tf_op jit(solution)/shard_map/ppermute | solution.py:19
  214.8 5.2 %collective-permute-done.10 = f32[8,1,64,128]{3,2,1,0:T(8,128)S(1)} collective-permute-done((f32[8,1,64,128]{3,2,1,0:T(8,128)S(1)}, f32[8,1,64,128]{3,2,1,0:T(8,128)S(1)}, u32[]{:S(2)}, u32[]{:S(2)}) %collective-permute-start.10) | collective-permute-done | bytes 262176 | tf_op jit(solution)/shard_map/ppermute | solution.py:17
  220.7 1.3 pad_maximum_fusion.2
  222.0 0.9 broadcast.33
  222.9 0.9 broadcast.33.clone
  223.8 68.2 %while.38 = (s32[]{:T(128)}, f32[36,32,128]{2,1,0:T(8,128)}, f32[36,32,128]{2,1,0:T(8,128)}, s32[]{:T(128)}, f32[36,9]{0,1:T(8,128)S(1)}, /*index=5*/s32[36,9]{0...) while((s32[]{:T(128)}, f32[36,32,128]{2,1,0:T(8,128)}, ...), condition=%wide.region_6.8_spmd, body=%wide.region_5.7_spmd.sunk | while | flops 454460640 | bytes 20059900 | solution.py:81
  225.3 4.0 %fusion.70 = f32[36,64,128]{2,1,0:T(8,128)S(1)} fusion(f32[36,9,128,128]{3,2,0,1:T(8,128)} %get-tuple-element.595, s32[]{:T(128)S(6)} %select_n.110, f32[36,64,128]{2,1,0:T(8,128)S(1)} %gather_fusion.2, pred[36]{0:T(512)(128)(4,1)S(1)} %get-tuple-element.487), kind=kOutput, calls=%fused_computation.41.clone.1 | convolution fusion | flops 453279744 | bytes 4718632 | tf_op jit(solution)/shard_map/while/body/npb,nba->npa/dot_general | solution.py:70
  232.8 4.0 %fusion.70 = f32[36,64,128]{2,1,0:T(8,128)S(1)} fusion(f32[36,9,128,128]{3,2,0,1:T(8,128)} %get-tuple-element.595, s32[]{:T(128)S(6)} %select_n.110, f32[36,64,128]{2,1,0:T(8,128)S(1)} %gather_fusion.2, pred[36]{0:T(512)(128)(4,1)S(1)} %get-tuple-element.487), kind=kOutput, calls=%fused_computation.41.clone.1 | convolution fusion | flops 453279744 | bytes 4718632 | tf_op jit(solution)/shard_map/while/body/npb,nba->npa/dot_general | solution.py:70
  240.3 4.0 %fusion.70 = f32[36,64,128]{2,1,0:T(8,128)S(1)} fusion(f32[36,9,128,128]{3,2,0,1:T(8,128)} %get-tuple-element.595, s32[]{:T(128)S(6)} %select_n.110, f32[36,64,128]{2,1,0:T(8,128)S(1)} %gather_fusion.2, pred[36]{0:T(512)(128)(4,1)S(1)} %get-tuple-element.487), kind=kOutput, calls=%fused_computation.41.clone.1 | convolution fusion | flops 453279744 | bytes 4718632 | tf_op jit(solution)/shard_map/while/body/npb,nba->npa/dot_general | solution.py:70
  247.8 4.0 %fusion.70 = f32[36,64,128]{2,1,0:T(8,128)S(1)} fusion(f32[36,9,128,128]{3,2,0,1:T(8,128)} %get-tuple-element.595, s32[]{:T(128)S(6)} %select_n.110, f32[36,64,128]{2,1,0:T(8,128)S(1)} %gather_fusion.2, pred[36]{0:T(512)(128)(4,1)S(1)} %get-tuple-element.487), kind=kOutput, calls=%fused_computation.41.clone.1 | convolution fusion | flops 453279744 | bytes 4718632 | tf_op jit(solution)/shard_map/while/body/npb,nba->npa/dot_general | solution.py:70
  255.3 4.0 %fusion.70 = f32[36,64,128]{2,1,0:T(8,128)S(1)} fusion(f32[36,9,128,128]{3,2,0,1:T(8,128)} %get-tuple-element.595, s32[]{:T(128)S(6)} %select_n.110, f32[36,64,128]{2,1,0:T(8,128)S(1)} %gather_fusion.2, pred[36]{0:T(512)(128)(4,1)S(1)} %get-tuple-element.487), kind=kOutput, calls=%fused_computation.41.clone.1 | convolution fusion | flops 453279744 | bytes 4718632 | tf_op jit(solution)/shard_map/while/body/npb,nba->npa/dot_general | solution.py:70
  262.8 4.0 %fusion.70 = f32[36,64,128]{2,1,0:T(8,128)S(1)} fusion(f32[36,9,128,128]{3,2,0,1:T(8,128)} %get-tuple-element.595, s32[]{:T(128)S(6)} %select_n.110, f32[36,64,128]{2,1,0:T(8,128)S(1)} %gather_fusion.2, pred[36]{0:T(512)(128)(4,1)S(1)} %get-tuple-element.487), kind=kOutput, calls=%fused_computation.41.clone.1 | convolution fusion | flops 453279744 | bytes 4718632 | tf_op jit(solution)/shard_map/while/body/npb,nba->npa/dot_general | solution.py:70
  270.3 4.0 %fusion.70 = f32[36,64,128]{2,1,0:T(8,128)S(1)} fusion(f32[36,9,128,128]{3,2,0,1:T(8,128)} %get-tuple-element.595, s32[]{:T(128)S(6)} %select_n.110, f32[36,64,128]{2,1,0:T(8,128)S(1)} %gather_fusion.2, pred[36]{0:T(512)(128)(4,1)S(1)} %get-tuple-element.487), kind=kOutput, calls=%fused_computation.41.clone.1 | convolution fusion | flops 453279744 | bytes 4718632 | tf_op jit(solution)/shard_map/while/body/npb,nba->npa/dot_general | solution.py:70
  277.7 4.0 %fusion.70 = f32[36,64,128]{2,1,0:T(8,128)S(1)} fusion(f32[36,9,128,128]{3,2,0,1:T(8,128)} %get-tuple-element.595, s32[]{:T(128)S(6)} %select_n.110, f32[36,64,128]{2,1,0:T(8,128)S(1)} %gather_fusion.2, pred[36]{0:T(512)(128)(4,1)S(1)} %get-tuple-element.487), kind=kOutput, calls=%fused_computation.41.clone.1 | convolution fusion | flops 453279744 | bytes 4718632 | tf_op jit(solution)/shard_map/while/body/npb,nba->npa/dot_general | solution.py:70
  285.2 4.0 %fusion.70 = f32[36,64,128]{2,1,0:T(8,128)S(1)} fusion(f32[36,9,128,128]{3,2,0,1:T(8,128)} %get-tuple-element.595, s32[]{:T(128)S(6)} %select_n.110, f32[36,64,128]{2,1,0:T(8,128)S(1)} %gather_fusion.2, pred[36]{0:T(512)(128)(4,1)S(1)} %get-tuple-element.487), kind=kOutput, calls=%fused_computation.41.clone.1 | convolution fusion | flops 453279744 | bytes 4718632 | tf_op jit(solution)/shard_map/while/body/npb,nba->npa/dot_general | solution.py:70
  292.0 1.4 maximum_multiply_fusion.1
  293.8 1.1 copy-done.16
  295.3 1.2 add_reduce_fusion.2
  296.5 39.2 %all-reduce = (f32[2,32]{1,0:T(2,128)S(1)}, f32[2,32]{1,0:T(2,128)S(1)}, f32[2,32]{1,0:T(2,128)S(1)}) all-reduce(f32[2,32]{1,0:T(2,128)S(1)} %pad_maximum_fusion.12, f32[2,32]{1,0:T(2,128)S(1)} %pad_maximum_fusion.11, f32[2,32]{1,0:T(2,128)S(1)} %pad_maximum_fusion.10), channel_id=1, replica_groups=mesh['gx'=4,'gy'=8] {'gx','gy'}, use_global_device_ids=true, to_apply=%region_15.17 | all-reduce | flops 192 | bytes 1536 | tf_op jit(solution)/shard_map/psum | solution.py:87
  (418 shorter events, 81.6 us)
Async XLA Ops:
  0.6 10.9 %copy-start.17 = (f32[6,6,64,128]{3,2,1,0:T(8,128)S(1)}, f32[6,6,64,128]{3,2,1,0:T(8,128)}, u32[]{:S(2)}) copy-start(f32[6,6,64,128]{3,2,1,0:T(8,128)} %param.14) | copy-start | bytes 3538948
  1.8 9.7 %collective-permute-start = (f32[1,6,64,128]{3,2,1,0:T(8,128)S(1)}, f32[1,6,64,128]{3,2,1,0:T(8,128)S(1)}, u32[]{:S(2)}, u32[]{:S(2)}) collective-permute-start(f32[1,6,64,128]{3,2,1,0:T(8,128)S(1)} %get-tuple-element.281), channel_id=1, source_target_pairs={{0,8},{8,16},{16,24},{24,0},{1,9},{9,17},{17,25},{25,1},{2,10},{10... | collective-permute-start | bytes 589832 | tf_op jit(solution)/shard_map/ppermute | solution.py:17
  4.8 10.3 %collective-permute-start.1 = (f32[1,6,64,128]{3,2,1,0:T(8,128)S(1)}, f32[1,6,64,128]{3,2,1,0:T(8,128)S(1)}, u32[]{:S(2)}, u32[]{:S(2)}) collective-permute-start(f32[1,6,64,128]{3,2,1,0:T(8,128)S(1)} %get-tuple-element.280), channel_id=1, source_target_pairs={{8,0},{16,8},{24,16},{0,24},{9,1},{17,9},{25,17},{1,25},{10,2},{18... | collective-permute-start | bytes 589832 | tf_op jit(solution)/shard_map/ppermute | solution.py:19
  11.6 8.6 %copy-start.26 = (s32[6,6,9]{2,1,0:T(8,128)S(1)}, s32[6,6,9]{2,1,0:T(8,128)}, u32[]{:S(2)}) copy-start(s32[6,6,9]{2,1,0:T(8,128)} %param.16) | copy-start | bytes 3892
  16.4 20.1 %collective-permute-start.2 = (f32[8,1,64,128]{3,2,1,0:T(8,128)S(1)}, f32[8,1,64,128]{3,2,1,0:T(8,128)S(1)}, u32[]{:S(2)}, u32[]{:S(2)}) collective-permute-start(f32[8,1,64,128]{3,2,1,0:T(8,128)S(1)} %get-tuple-element.272), channel_id=1, source_target_pairs={{0,1},{1,2},{2,3},{3,4},{4,5},{5,6},{6,7},{7,0},{8,9},{9,10},{10,1... | collective-permute-start | bytes 786440 | tf_op jit(solution)/shard_map/ppermute | solution.py:17
  16.5 20.1 %collective-permute-start.3 = (f32[8,1,64,128]{3,2,1,0:T(8,128)S(1)}, f32[8,1,64,128]{3,2,1,0:T(8,128)S(1)}, u32[]{:S(2)}, u32[]{:S(2)}) collective-permute-start(f32[8,1,64,128]{3,2,1,0:T(8,128)S(1)} %get-tuple-element.273), channel_id=1, source_target_pairs={{1,0},{2,1},{3,2},{4,3},{5,4},{6,5},{7,6},{0,7},{9,8},{10,9},{11,1... | collective-permute-start | bytes 786440 | tf_op jit(solution)/shard_map/ppermute | solution.py:19
  20.4 15.5 %copy-start.27 = (s32[6,6]{1,0:T(8,128)S(1)}, s32[6,6]{1,0:T(8,128)}, u32[]{:S(2)}) copy-start(s32[6,6]{1,0:T(8,128)} %param.18) | copy-start | bytes 436
  41.2 4.1 %copy-start.4 = (f32[36,32,128]{2,1,0:T(8,128)S(1)}, f32[36,32,128]{2,1,0:T(8,128)}, u32[]{:S(2)}) copy-start(f32[36,32,128]{2,1,0:T(8,128)} %get-tuple-element.505) | copy-start | bytes 1769476 | tf_op jit(solution)/shard_map/while
  41.2 4.1 %copy-start.6 = (f32[36,32,128]{2,1,0:T(8,128)S(1)}, f32[36,32,128]{2,1,0:T(8,128)}, u32[]{:S(2)}) copy-start(f32[36,32,128]{2,1,0:T(8,128)} %get-tuple-element.506) | copy-start | bytes 1769476 | tf_op jit(solution)/shard_map/while
  48.6 4.1 %copy-start.4 = (f32[36,32,128]{2,1,0:T(8,128)S(1)}, f32[36,32,128]{2,1,0:T(8,128)}, u32[]{:S(2)}) copy-start(f32[36,32,128]{2,1,0:T(8,128)} %get-tuple-element.505) | copy-start | bytes 1769476 | tf_op jit(solution)/shard_map/while
  48.6 4.1 %copy-start.6 = (f32[36,32,128]{2,1,0:T(8,128)S(1)}, f32[36,32,128]{2,1,0:T(8,128)}, u32[]{:S(2)}) copy-start(f32[36,32,128]{2,1,0:T(8,128)} %get-tuple-element.506) | copy-start | bytes 1769476 | tf_op jit(solution)/shard_map/while
  56.1 4.1 %copy-start.4 = (f32[36,32,128]{2,1,0:T(8,128)S(1)}, f32[36,32,128]{2,1,0:T(8,128)}, u32[]{:S(2)}) copy-start(f32[36,32,128]{2,1,0:T(8,128)} %get-tuple-element.505) | copy-start | bytes 1769476 | tf_op jit(solution)/shard_map/while
  56.1 4.1 %copy-start.6 = (f32[36,32,128]{2,1,0:T(8,128)S(1)}, f32[36,32,128]{2,1,0:T(8,128)}, u32[]{:S(2)}) copy-start(f32[36,32,128]{2,1,0:T(8,128)} %get-tuple-element.506) | copy-start | bytes 1769476 | tf_op jit(solution)/shard_map/while
  63.5 4.1 %copy-start.4 = (f32[36,32,128]{2,1,0:T(8,128)S(1)}, f32[36,32,128]{2,1,0:T(8,128)}, u32[]{:S(2)}) copy-start(f32[36,32,128]{2,1,0:T(8,128)} %get-tuple-element.505) | copy-start | bytes 1769476 | tf_op jit(solution)/shard_map/while
  63.5 4.1 %copy-start.6 = (f32[36,32,128]{2,1,0:T(8,128)S(1)}, f32[36,32,128]{2,1,0:T(8,128)}, u32[]{:S(2)}) copy-start(f32[36,32,128]{2,1,0:T(8,128)} %get-tuple-element.506) | copy-start | bytes 1769476 | tf_op jit(solution)/shard_map/while
  71.0 4.1 %copy-start.4 = (f32[36,32,128]{2,1,0:T(8,128)S(1)}, f32[36,32,128]{2,1,0:T(8,128)}, u32[]{:S(2)}) copy-start(f32[36,32,128]{2,1,0:T(8,128)} %get-tuple-element.505) | copy-start | bytes 1769476 | tf_op jit(solution)/shard_map/while
  71.0 4.1 %copy-start.6 = (f32[36,32,128]{2,1,0:T(8,128)S(1)}, f32[36,32,128]{2,1,0:T(8,128)}, u32[]{:S(2)}) copy-start(f32[36,32,128]{2,1,0:T(8,128)} %get-tuple-element.506) | copy-start | bytes 1769476 | tf_op jit(solution)/shard_map/while
  78.4 4.1 %copy-start.4 = (f32[36,32,128]{2,1,0:T(8,128)S(1)}, f32[36,32,128]{2,1,0:T(8,128)}, u32[]{:S(2)}) copy-start(f32[36,32,128]{2,1,0:T(8,128)} %get-tuple-element.505) | copy-start | bytes 1769476 | tf_op jit(solution)/shard_map/while
  78.4 4.1 %copy-start.6 = (f32[36,32,128]{2,1,0:T(8,128)S(1)}, f32[36,32,128]{2,1,0:T(8,128)}, u32[]{:S(2)}) copy-start(f32[36,32,128]{2,1,0:T(8,128)} %get-tuple-element.506) | copy-start | bytes 1769476 | tf_op jit(solution)/shard_map/while
  85.8 4.1 %copy-start.4 = (f32[36,32,128]{2,1,0:T(8,128)S(1)}, f32[36,32,128]{2,1,0:T(8,128)}, u32[]{:S(2)}) copy-start(f32[36,32,128]{2,1,0:T(8,128)} %get-tuple-element.505) | copy-start | bytes 1769476 | tf_op jit(solution)/shard_map/while
  85.8 4.1 %copy-start.6 = (f32[36,32,128]{2,1,0:T(8,128)S(1)}, f32[36,32,128]{2,1,0:T(8,128)}, u32[]{:S(2)}) copy-start(f32[36,32,128]{2,1,0:T(8,128)} %get-tuple-element.506) | copy-start | bytes 1769476 | tf_op jit(solution)/shard_map/while
  93.3 4.1 %copy-start.4 = (f32[36,32,128]{2,1,0:T(8,128)S(1)}, f32[36,32,128]{2,1,0:T(8,128)}, u32[]{:S(2)}) copy-start(f32[36,32,128]{2,1,0:T(8,128)} %get-tuple-element.505) | copy-start | bytes 1769476 | tf_op jit(solution)/shard_map/while
  93.3 4.1 %copy-start.6 = (f32[36,32,128]{2,1,0:T(8,128)S(1)}, f32[36,32,128]{2,1,0:T(8,128)}, u32[]{:S(2)}) copy-start(f32[36,32,128]{2,1,0:T(8,128)} %get-tuple-element.506) | copy-start | bytes 1769476 | tf_op jit(solution)/shard_map/while
  100.7 4.1 %copy-start.4 = (f32[36,32,128]{2,1,0:T(8,128)S(1)}, f32[36,32,128]{2,1,0:T(8,128)}, u32[]{:S(2)}) copy-start(f32[36,32,128]{2,1,0:T(8,128)} %get-tuple-element.505) | copy-start | bytes 1769476 | tf_op jit(solution)/shard_map/while
  100.7 4.1 %copy-start.6 = (f32[36,32,128]{2,1,0:T(8,128)S(1)}, f32[36,32,128]{2,1,0:T(8,128)}, u32[]{:S(2)}) copy-start(f32[36,32,128]{2,1,0:T(8,128)} %get-tuple-element.506) | copy-start | bytes 1769476 | tf_op jit(solution)/shard_map/while
  108.8 19.9 %copy-start.13 = (f32[36,64,128]{2,1,0:T(8,128)}, f32[36,64,128]{2,1,0:T(8,128)S(1)}, u32[]{:S(2)}) copy-start(f32[36,64,128]{2,1,0:T(8,128)S(1)} %constant_dynamic-update-slice_fusion.3) | copy-start | bytes 3538948
  108.8 8.0 %collective-permute-start.4 = (f32[1,6,64,128]{3,2,1,0:T(8,128)S(1)}, f32[1,6,64,128]{3,2,1,0:T(8,128)S(1)}, u32[]{:S(2)}, u32[]{:S(2)}) collective-permute-start(f32[1,6,64,128]{3,2,1,0:T(8,128)S(1)} %get-tuple-element.278), channel_id=1, source_target_pairs={{0,8},{8,16},{16,24},{24,0},{1,9},{9,17},{17,25},{25,1},{2,10},{10... | collective-permute-start | bytes 589832 | tf_op jit(solution)/shard_map/ppermute | solution.py:17
  110.4 7.4 %collective-permute-start.5 = (f32[1,6,64,128]{3,2,1,0:T(8,128)S(1)}, f32[1,6,64,128]{3,2,1,0:T(8,128)S(1)}, u32[]{:S(2)}, u32[]{:S(2)}) collective-permute-start(f32[1,6,64,128]{3,2,1,0:T(8,128)S(1)} %get-tuple-element.279), channel_id=1, source_target_pairs={{8,0},{16,8},{24,16},{0,24},{9,1},{17,9},{25,17},{1,25},{10,2},{18... | collective-permute-start | bytes 589832 | tf_op jit(solution)/shard_map/ppermute | solution.py:19
  118.5 9.4 %collective-permute-start.6 = (f32[8,1,64,128]{3,2,1,0:T(8,128)S(1)}, f32[8,1,64,128]{3,2,1,0:T(8,128)S(1)}, u32[]{:S(2)}, u32[]{:S(2)}) collective-permute-start(f32[8,1,64,128]{3,2,1,0:T(8,128)S(1)} %get-tuple-element.270), channel_id=1, source_target_pairs={{0,1},{1,2},{2,3},{3,4},{4,5},{5,6},{6,7},{7,0},{8,9},{9,10},{10,1... | collective-permute-start | bytes 786440 | tf_op jit(solution)/shard_map/ppermute | solution.py:17
  118.6 10.0 %collective-permute-start.7 = (f32[8,1,64,128]{3,2,1,0:T(8,128)S(1)}, f32[8,1,64,128]{3,2,1,0:T(8,128)}, u32[]{:S(2)}, u32[]{:S(2)}) collective-permute-start(f32[8,1,64,128]{3,2,1,0:T(8,128)S(1)} %get-tuple-element.271), channel_id=1, source_target_pairs={{1,0},{2,1},{3,2},{4,3},{5,4},{6,5},{7,6},{0,7},{9,8},{10,9},{11,1... | collective-permute-start | bytes 786440 | tf_op jit(solution)/shard_map/ppermute | solution.py:19
  133.1 4.1 %copy-start.9 = (f32[36,32,128]{2,1,0:T(8,128)S(1)}, f32[36,32,128]{2,1,0:T(8,128)}, u32[]{:S(2)}) copy-start(f32[36,32,128]{2,1,0:T(8,128)} %get-tuple-element.541) | copy-start | bytes 1769476 | tf_op jit(solution)/shard_map/while
  133.1 4.1 %copy-start.11 = (f32[36,32,128]{2,1,0:T(8,128)S(1)}, f32[36,32,128]{2,1,0:T(8,128)}, u32[]{:S(2)}) copy-start(f32[36,32,128]{2,1,0:T(8,128)} %get-tuple-element.542) | copy-start | bytes 1769476 | tf_op jit(solution)/shard_map/while
  140.5 4.1 %copy-start.9 = (f32[36,32,128]{2,1,0:T(8,128)S(1)}, f32[36,32,128]{2,1,0:T(8,128)}, u32[]{:S(2)}) copy-start(f32[36,32,128]{2,1,0:T(8,128)} %get-tuple-element.541) | copy-start | bytes 1769476 | tf_op jit(solution)/shard_map/while
  140.5 4.1 %copy-start.11 = (f32[36,32,128]{2,1,0:T(8,128)S(1)}, f32[36,32,128]{2,1,0:T(8,128)}, u32[]{:S(2)}) copy-start(f32[36,32,128]{2,1,0:T(8,128)} %get-tuple-element.542) | copy-start | bytes 1769476 | tf_op jit(solution)/shard_map/while
  147.9 4.1 %copy-start.9 = (f32[36,32,128]{2,1,0:T(8,128)S(1)}, f32[36,32,128]{2,1,0:T(8,128)}, u32[]{:S(2)}) copy-start(f32[36,32,128]{2,1,0:T(8,128)} %get-tuple-element.541) | copy-start | bytes 1769476 | tf_op jit(solution)/shard_map/while
  148.0 4.1 %copy-start.11 = (f32[36,32,128]{2,1,0:T(8,128)S(1)}, f32[36,32,128]{2,1,0:T(8,128)}, u32[]{:S(2)}) copy-start(f32[36,32,128]{2,1,0:T(8,128)} %get-tuple-element.542) | copy-start | bytes 1769476 | tf_op jit(solution)/shard_map/while
  155.4 4.1 %copy-start.9 = (f32[36,32,128]{2,1,0:T(8,128)S(1)}, f32[36,32,128]{2,1,0:T(8,128)}, u32[]{:S(2)}) copy-start(f32[36,32,128]{2,1,0:T(8,128)} %get-tuple-element.541) | copy-start | bytes 1769476 | tf_op jit(solution)/shard_map/while
  155.4 4.1 %copy-start.11 = (f32[36,32,128]{2,1,0:T(8,128)S(1)}, f32[36,32,128]{2,1,0:T(8,128)}, u32[]{:S(2)}) copy-start(f32[36,32,128]{2,1,0:T(8,128)} %get-tuple-element.542) | copy-start | bytes 1769476 | tf_op jit(solution)/shard_map/while
  162.8 4.1 %copy-start.9 = (f32[36,32,128]{2,1,0:T(8,128)S(1)}, f32[36,32,128]{2,1,0:T(8,128)}, u32[]{:S(2)}) copy-start(f32[36,32,128]{2,1,0:T(8,128)} %get-tuple-element.541) | copy-start | bytes 1769476 | tf_op jit(solution)/shard_map/while
  162.8 4.1 %copy-start.11 = (f32[36,32,128]{2,1,0:T(8,128)S(1)}, f32[36,32,128]{2,1,0:T(8,128)}, u32[]{:S(2)}) copy-start(f32[36,32,128]{2,1,0:T(8,128)} %get-tuple-element.542) | copy-start | bytes 1769476 | tf_op jit(solution)/shard_map/while
  170.3 4.1 %copy-start.9 = (f32[36,32,128]{2,1,0:T(8,128)S(1)}, f32[36,32,128]{2,1,0:T(8,128)}, u32[]{:S(2)}) copy-start(f32[36,32,128]{2,1,0:T(8,128)} %get-tuple-element.541) | copy-start | bytes 1769476 | tf_op jit(solution)/shard_map/while
  170.3 4.1 %copy-start.11 = (f32[36,32,128]{2,1,0:T(8,128)S(1)}, f32[36,32,128]{2,1,0:T(8,128)}, u32[]{:S(2)}) copy-start(f32[36,32,128]{2,1,0:T(8,128)} %get-tuple-element.542) | copy-start | bytes 1769476 | tf_op jit(solution)/shard_map/while
  177.7 4.1 %copy-start.9 = (f32[36,32,128]{2,1,0:T(8,128)S(1)}, f32[36,32,128]{2,1,0:T(8,128)}, u32[]{:S(2)}) copy-start(f32[36,32,128]{2,1,0:T(8,128)} %get-tuple-element.541) | copy-start | bytes 1769476 | tf_op jit(solution)/shard_map/while
  177.7 4.1 %copy-start.11 = (f32[36,32,128]{2,1,0:T(8,128)S(1)}, f32[36,32,128]{2,1,0:T(8,128)}, u32[]{:S(2)}) copy-start(f32[36,32,128]{2,1,0:T(8,128)} %get-tuple-element.542) | copy-start | bytes 1769476 | tf_op jit(solution)/shard_map/while
  185.1 4.1 %copy-start.9 = (f32[36,32,128]{2,1,0:T(8,128)S(1)}, f32[36,32,128]{2,1,0:T(8,128)}, u32[]{:S(2)}) copy-start(f32[36,32,128]{2,1,0:T(8,128)} %get-tuple-element.541) | copy-start | bytes 1769476 | tf_op jit(solution)/shard_map/while
  192.6 4.1 %copy-start.9 = (f32[36,32,128]{2,1,0:T(8,128)S(1)}, f32[36,32,128]{2,1,0:T(8,128)}, u32[]{:S(2)}) copy-start(f32[36,32,128]{2,1,0:T(8,128)} %get-tuple-element.541) | copy-start | bytes 1769476 | tf_op jit(solution)/shard_map/while
  192.6 4.1 %copy-start.11 = (f32[36,32,128]{2,1,0:T(8,128)S(1)}, f32[36,32,128]{2,1,0:T(8,128)}, u32[]{:S(2)}) copy-start(f32[36,32,128]{2,1,0:T(8,128)} %get-tuple-element.542) | copy-start | bytes 1769476 | tf_op jit(solution)/shard_map/while
  201.1 19.5 %copy-start.15 = (f32[6,6,64,128]{3,2,1,0:T(8,128)}, f32[6,6,64,128]{3,2,1,0:T(8,128)S(1)}, u32[]{:S(2)}) copy-start(f32[6,6,64,128]{3,2,1,0:T(8,128)S(1)} %sub.47) | copy-start | bytes 3538948
  201.2 8.7 %collective-permute-start.8 = (f32[1,6,64,128]{3,2,1,0:T(8,128)S(1)}, f32[1,6,64,128]{3,2,1,0:T(8,128)S(1)}, u32[]{:S(2)}, u32[]{:S(2)}) collective-permute-start(f32[1,6,64,128]{3,2,1,0:T(8,128)S(1)} %get-tuple-element.276), channel_id=1, source_target_pairs={{0,8},{8,16},{16,24},{24,0},{1,9},{9,17},{17,25},{25,1},{2,10},{10... | collective-permute-start | bytes 589832 | tf_op jit(solution)/shard_map/ppermute | solution.py:17
  201.3 9.2 %collective-permute-start.9 = (f32[1,6,64,128]{3,2,1,0:T(8,128)S(1)}, f32[1,6,64,128]{3,2,1,0:T(8,128)S(1)}, u32[]{:S(2)}, u32[]{:S(2)}) collective-permute-start(f32[1,6,64,128]{3,2,1,0:T(8,128)S(1)} %get-tuple-element.277), channel_id=1, source_target_pairs={{8,0},{16,8},{24,16},{0,24},{9,1},{17,9},{25,17},{1,25},{10,2},{18... | collective-permute-start | bytes 589832 | tf_op jit(solution)/shard_map/ppermute | solution.py:19
  211.2 8.8 %collective-permute-start.10 = (f32[8,1,64,128]{3,2,1,0:T(8,128)S(1)}, f32[8,1,64,128]{3,2,1,0:T(8,128)S(1)}, u32[]{:S(2)}, u32[]{:S(2)}) collective-permute-start(f32[8,1,64,128]{3,2,1,0:T(8,128)S(1)} %get-tuple-element.268), channel_id=1, source_target_pairs={{0,1},{1,2},{2,3},{3,4},{4,5},{5,6},{6,7},{7,0},{8,9},{9,10},{10,1... | collective-permute-start | bytes 786440 | tf_op jit(solution)/shard_map/ppermute | solution.py:17
  211.3 9.4 %collective-permute-start.11 = (f32[8,1,64,128]{3,2,1,0:T(8,128)S(1)}, f32[8,1,64,128]{3,2,1,0:T(8,128)}, u32[]{:S(2)}, u32[]{:S(2)}) collective-permute-start(f32[8,1,64,128]{3,2,1,0:T(8,128)S(1)} %get-tuple-element.269), channel_id=1, source_target_pairs={{1,0},{2,1},{3,2},{4,3},{5,4},{6,5},{7,6},{0,7},{9,8},{10,9},{11,1... | collective-permute-start | bytes 786440 | tf_op jit(solution)/shard_map/ppermute | solution.py:19
  240.3 4.1 %copy-start = (f32[36,32,128]{2,1,0:T(8,128)S(1)}, f32[36,32,128]{2,1,0:T(8,128)}, u32[]{:S(2)}) copy-start(f32[36,32,128]{2,1,0:T(8,128)} %get-tuple-element.577) | copy-start | bytes 1769476 | tf_op jit(solution)/shard_map/while
  240.3 4.1 %copy-start.2 = (f32[36,32,128]{2,1,0:T(8,128)S(1)}, f32[36,32,128]{2,1,0:T(8,128)}, u32[]{:S(2)}) copy-start(f32[36,32,128]{2,1,0:T(8,128)} %get-tuple-element.578) | copy-start | bytes 1769476 | tf_op jit(solution)/shard_map/while
  247.8 4.1 %copy-start = (f32[36,32,128]{2,1,0:T(8,128)S(1)}, f32[36,32,128]{2,1,0:T(8,128)}, u32[]{:S(2)}) copy-start(f32[36,32,128]{2,1,0:T(8,128)} %get-tuple-element.577) | copy-start | bytes 1769476 | tf_op jit(solution)/shard_map/while
  247.8 4.1 %copy-start.2 = (f32[36,32,128]{2,1,0:T(8,128)S(1)}, f32[36,32,128]{2,1,0:T(8,128)}, u32[]{:S(2)}) copy-start(f32[36,32,128]{2,1,0:T(8,128)} %get-tuple-element.578) | copy-start | bytes 1769476 | tf_op jit(solution)/shard_map/while
  255.3 4.1 %copy-start = (f32[36,32,128]{2,1,0:T(8,128)S(1)}, f32[36,32,128]{2,1,0:T(8,128)}, u32[]{:S(2)}) copy-start(f32[36,32,128]{2,1,0:T(8,128)} %get-tuple-element.577) | copy-start | bytes 1769476 | tf_op jit(solution)/shard_map/while
  255.3 4.1 %copy-start.2 = (f32[36,32,128]{2,1,0:T(8,128)S(1)}, f32[36,32,128]{2,1,0:T(8,128)}, u32[]{:S(2)}) copy-start(f32[36,32,128]{2,1,0:T(8,128)} %get-tuple-element.578) | copy-start | bytes 1769476 | tf_op jit(solution)/shard_map/while
  262.8 4.1 %copy-start = (f32[36,32,128]{2,1,0:T(8,128)S(1)}, f32[36,32,128]{2,1,0:T(8,128)}, u32[]{:S(2)}) copy-start(f32[36,32,128]{2,1,0:T(8,128)} %get-tuple-element.577) | copy-start | bytes 1769476 | tf_op jit(solution)/shard_map/while
  262.8 4.1 %copy-start.2 = (f32[36,32,128]{2,1,0:T(8,128)S(1)}, f32[36,32,128]{2,1,0:T(8,128)}, u32[]{:S(2)}) copy-start(f32[36,32,128]{2,1,0:T(8,128)} %get-tuple-element.578) | copy-start | bytes 1769476 | tf_op jit(solution)/shard_map/while
  270.2 4.1 %copy-start = (f32[36,32,128]{2,1,0:T(8,128)S(1)}, f32[36,32,128]{2,1,0:T(8,128)}, u32[]{:S(2)}) copy-start(f32[36,32,128]{2,1,0:T(8,128)} %get-tuple-element.577) | copy-start | bytes 1769476 | tf_op jit(solution)/shard_map/while
  270.2 4.1 %copy-start.2 = (f32[36,32,128]{2,1,0:T(8,128)S(1)}, f32[36,32,128]{2,1,0:T(8,128)}, u32[]{:S(2)}) copy-start(f32[36,32,128]{2,1,0:T(8,128)} %get-tuple-element.578) | copy-start | bytes 1769476 | tf_op jit(solution)/shard_map/while
  277.7 4.1 %copy-start = (f32[36,32,128]{2,1,0:T(8,128)S(1)}, f32[36,32,128]{2,1,0:T(8,128)}, u32[]{:S(2)}) copy-start(f32[36,32,128]{2,1,0:T(8,128)} %get-tuple-element.577) | copy-start | bytes 1769476 | tf_op jit(solution)/shard_map/while
  277.7 4.1 %copy-start.2 = (f32[36,32,128]{2,1,0:T(8,128)S(1)}, f32[36,32,128]{2,1,0:T(8,128)}, u32[]{:S(2)}) copy-start(f32[36,32,128]{2,1,0:T(8,128)} %get-tuple-element.578) | copy-start | bytes 1769476 | tf_op jit(solution)/shard_map/while
  (72 other events, 85.5 us)
where the time goes:
time: 337 us; the launch traced here: 336 us
  matrix products  108 us (32%)
  local copies, waits for them, and re-layouts  93.3 us (28%)
  blocking collectives  39.2 us (12%)
  waiting for transfers between devices  27.5 us (8%)
  other arithmetic  24.5 us (7%)
  loops' own time  21.9 us (6%)
  starting transfers between devices  20.8 us (6%)
    dot_general x27, matrix products, accumulate(): jnp.einsum('npb,nba->npa', piece, chosen, precision=lax.Precision.HIGHEST)  108 us
    while x216, local copies, waits for them, and re-layouts  44.5 us
    psum x1, blocking collectives, reduce_one(): return lax.psum(intersection(probes, field), ('gx', 'gy')) * scale  39.2 us
    unnamed x36, local copies, waits for them, and re-layouts  22.6 us
    ppermute x6, waiting for transfers between devices, with_halo(): lax.ppermute(tail, axis, [(i, (i + 1) % count) for i in range(count)])  22.5 us
    another operation x3, loops' own time, apply_hamiltonian(): lax.fori_loop(0, slot_bound, accumulate, (zeros, zeros))  21.9 us
    gather x27, local copies, waits for them, and re-layouts, accumulate(): piece = jnp.take(source, flat_partner[:, slot], axis=0)  16.9 us
    ppermute x6, starting transfers between devices, with_halo(): lax.ppermute(head, axis, [((i + 1) % count, i) for i in range(count)])  16 us
  transfers between devices with their start and end apart: 12, of which 8 were waited for; matrix products, arithmetic and copies ran while one was open for 6% of the time, Pallas kernels for 0%

commit v1 on v0

--- a/solution.py
+++ b/solution.py
@@ -84,7 +84,7 @@
     scale = 1.0 / math.sqrt(total_x * total_y * block)
 
     def reduce_one(field):
-        return lax.psum(intersection(probes, field), ("gx", "gy")) * scale
+        return jnp.sum(lax.all_gather(intersection(probes, field), ("gx", "gy")), axis=0) * scale
 
     before = probes
     current = apply_hamiltonian(probes)

time: 337 us -> 412 us (1.22)
  blocking collectives: 39.2 us -> 112 us
    all_gather x0 -> x3, blocking collectives: none -> 112 us  [reduce_one(): lax.all_gather(intersection(probes, field), ('gx', 'gy'))]
    psum x1 -> x0, blocking collectives: 39.2 us -> none  [reduce_one(): return lax.psum(intersection(probes, field), ('gx', 'gy')) * scale]
  transfers between devices with their start and end apart: 12 -> 12, of which waited for: 8 -> 8; matrix products, arithmetic and copies ran while one was open for 6% -> 5% of each run, Pallas kernels for 0% -> 0%
where the time goes in v1:
time: 412 us; the launch traced here: 409 us
  blocking collectives  112 us (27%)
  matrix products  108 us (26%)
  local copies, waits for them, and re-layouts  93.8 us (23%)
  waiting for transfers between devices  27.5 us (7%)
  other arithmetic  24.6 us (6%)
  loops' own time  21.2 us (5%)
  starting transfers between devices  20.8 us (5%)
    all_gather x3, blocking collectives, reduce_one(): lax.all_gather(intersection(probes, field), ('gx', 'gy'))  112 us
    dot_general x27, matrix products, accumulate(): jnp.einsum('npb,nba->npa', piece, chosen, precision=lax.Precision.HIGHEST)  108 us
    while x216, local copies, waits for them, and re-layouts  45 us
    ppermute x6, waiting for transfers between devices, with_halo(): lax.ppermute(tail, axis, [(i, (i + 1) % count) for i in range(count)])  22.5 us
    unnamed x36, local copies, waits for them, and re-layouts  22.5 us
    another operation x3, loops' own time, apply_hamiltonian(): lax.fori_loop(0, slot_bound, accumulate, (zeros, zeros))  21.2 us
    gather x27, local copies, waits for them, and re-layouts, accumulate(): piece = jnp.take(source, flat_partner[:, slot], axis=0)  16.9 us
    ppermute x6, starting transfers between devices, with_halo(): lax.ppermute(head, axis, [((i + 1) % count, i) for i in range(count)])  16 us
  transfers between devices with their start and end apart: 12, of which 8 were waited for; matrix products, arithmetic and copies ran while one was open for 5% of the time, Pallas kernels for 0%

profile of v1, /device:TPU:0, one launch (start us, length us, event | category | flops | bytes accessed | tf_op | source)
XLA Modules:
  0.0 408.7 jit_solution(12544108775933876293)
XLA Ops:
  0.6 1.1 fusion.46
  1.8 3.0 collective-permute-start
  4.8 1.0 collective-permute-start.1
  5.8 1.3 fusion.47
  7.1 2.8 sine_reduce_fusion
  11.6 3.5 collective-permute-done.1
  15.2 1.2 copy-done.21
  16.4 3.5 collective-permute-start.3
  20.4 15.4 %copy.22 = f32[6,6,9,128,128]{4,3,1,0,2:T(8,128)} copy(f32[6,6,9,128,128]{4,3,2,1,0:T(8,128)} %param.15) | data formatting | bytes 42467328 | tf_op args[1]
  36.5 1.6 pad_maximum_fusion
  38.9 0.9 broadcast.58.clone.4
  39.8 67.5 %while.36 = (s32[]{:T(128)}, f32[36,32,128]{2,1,0:T(8,128)}, f32[36,32,128]{2,1,0:T(8,128)}, s32[]{:T(128)}, f32[36,9]{0,1:T(8,128)S(1)}, /*index=5*/s32[36,9]{0...) while((s32[]{:T(128)}, f32[36,32,128]{2,1,0:T(8,128)}, ...), condition=%wide.region_2.4_spmd, body=%wide.region_1.3_spmd.sunk | while | flops 454460640 | bytes 20059900 | solution.py:81
  41.1 4.0 fusion.62
  48.6 4.0 fusion.62
  56.0 4.0 fusion.62
  63.4 4.0 fusion.62
  70.9 4.0 fusion.62
  78.3 4.0 fusion.62
  85.7 4.0 fusion.62
  93.2 4.0 fusion.62
  100.6 4.0 fusion.62
  107.4 1.2 constant_dynamic-update-slice_fusion.4
  108.7 1.5 collective-permute-start.4
  110.2 1.4 collective-permute-start.5
  111.7 5.0 %collective-permute-done.4 = f32[1,6,64,128]{3,2,1,0:T(8,128)S(1)} collective-permute-done((f32[1,6,64,128]{3,2,1,0:T(8,128)S(1)}, f32[1,6,64,128]{3,2,1,0:T(8,128)S(1)}, u32[]{:S(2)}, u32[]{:S(2)}) %collective-permute-start.4) | collective-permute-done | bytes 196640 | tf_op jit(solution)/shard_map/ppermute | solution.py:17
  116.7 1.0 collective-permute-done.5
  118.5 3.5 collective-permute-start.7
  122.0 5.8 %collective-permute-done.6 = f32[8,1,64,128]{3,2,1,0:T(8,128)S(1)} collective-permute-done((f32[8,1,64,128]{3,2,1,0:T(8,128)S(1)}, f32[8,1,64,128]{3,2,1,0:T(8,128)S(1)}, u32[]{:S(2)}, u32[]{:S(2)}) %collective-permute-start.6) | collective-permute-done | bytes 262176 | tf_op jit(solution)/shard_map/ppermute | solution.py:17
  128.5 1.3 pad_maximum_fusion.1
  129.8 0.9 broadcast.58.clone.1
  130.7 0.9 broadcast.58.clone.2
  131.6 67.8 %while.37 = (s32[]{:T(128)}, f32[36,32,128]{2,1,0:T(8,128)}, f32[36,32,128]{2,1,0:T(8,128)}, s32[]{:T(128)}, f32[36,9]{0,1:T(8,128)S(1)}, /*index=5*/s32[36,9]{0...) while((s32[]{:T(128)}, f32[36,32,128]{2,1,0:T(8,128)}, ...), condition=%wide.region_4.6_spmd, body=%wide.region_3.5_spmd.sunk | while | flops 454460640 | bytes 20059900 | solution.py:81
  133.0 4.0 fusion.66
  140.4 4.0 fusion.66
  147.9 4.0 fusion.66
  155.4 4.0 fusion.66
  162.8 4.0 fusion.66
  170.3 4.0 fusion.66
  177.8 4.0 fusion.66
  185.2 4.0 fusion.66
  192.7 4.0 fusion.66
  199.5 1.4 maximum_multiply_fusion
  201.4 2.9 collective-permute-start.9
  204.3 5.7 %collective-permute-done.8 = f32[1,6,64,128]{3,2,1,0:T(8,128)S(1)} collective-permute-done((f32[1,6,64,128]{3,2,1,0:T(8,128)S(1)}, f32[1,6,64,128]{3,2,1,0:T(8,128)S(1)}, u32[]{:S(2)}, u32[]{:S(2)}) %collective-permute-start.8) | collective-permute-done | bytes 196640 | tf_op jit(solution)/shard_map/ppermute | solution.py:17
  211.4 3.5 collective-permute-start.11
  214.9 5.2 %collective-permute-done.10 = f32[8,1,64,128]{3,2,1,0:T(8,128)S(1)} collective-permute-done((f32[8,1,64,128]{3,2,1,0:T(8,128)S(1)}, f32[8,1,64,128]{3,2,1,0:T(8,128)S(1)}, u32[]{:S(2)}, u32[]{:S(2)}) %collective-permute-start.10) | collective-permute-done | bytes 262176 | tf_op jit(solution)/shard_map/ppermute | solution.py:17
  220.8 1.3 pad_maximum_fusion.2
  222.1 0.9 broadcast.58
  223.9 67.8 %while.38 = (s32[]{:T(128)}, f32[36,32,128]{2,1,0:T(8,128)}, f32[36,32,128]{2,1,0:T(8,128)}, s32[]{:T(128)}, f32[36,9]{0,1:T(8,128)S(1)}, /*index=5*/s32[36,9]{0...) while((s32[]{:T(128)}, f32[36,32,128]{2,1,0:T(8,128)}, ...), condition=%wide.region_6.8_spmd, body=%wide.region_5.7_spmd.sunk | while | flops 454460640 | bytes 20059900 | solution.py:81
  225.4 4.0 fusion.70
  232.9 4.0 fusion.70
  240.3 4.0 fusion.70
  247.8 4.0 fusion.70
  255.2 4.0 fusion.70
  262.7 4.0 fusion.70
  270.1 4.0 fusion.70
  277.6 4.0 fusion.70
  285.0 4.0 fusion.70
  291.8 1.4 maximum_multiply_fusion.1
  293.6 1.1 copy-done.16
  295.0 1.2 add_reduce_fusion.2
  296.3 36.5 %all-gather.3 = f32[32,2,32]{2,1,0:T(2,128)S(1)} all-gather(f32[1,2,32]{2,1,0:T(2,128)S(1)} %maximum_bitcast_fusion), channel_id=2, replica_groups=mesh['gx'=4,'gy'=8] {'gx','gy'}, dimensions={0}, use_global_device_ids=true | all-gather | bytes 8448 | tf_op jit(solution)/shard_map/all_gather | solution.py:87
  332.8 38.4 %all-gather.4 = f32[32,2,32]{2,1,0:T(2,128)S(1)} all-gather(f32[1,2,32]{2,1,0:T(2,128)S(1)} %maximum_bitcast_fusion.1), channel_id=3, replica_groups=mesh['gx'=4,'gy'=8] {'gx','gy'}, dimensions={0}, use_global_device_ids=true | all-gather | bytes 8448 | tf_op jit(solution)/shard_map/all_gather | solution.py:87
  371.3 36.8 %all-gather.5 = f32[32,2,32]{2,1,0:T(2,128)S(1)} all-gather(f32[1,2,32]{2,1,0:T(2,128)S(1)} %maximum_bitcast_fusion.2), channel_id=4, replica_groups=mesh['gx'=4,'gy'=8] {'gx','gy'}, dimensions={0}, use_global_device_ids=true | all-gather | bytes 8448 | tf_op jit(solution)/shard_map/all_gather | solution.py:87
  (424 shorter events, 84.0 us)
Async XLA Ops:
  0.6 10.9 %copy-start.17 = (f32[6,6,64,128]{3,2,1,0:T(8,128)S(1)}, f32[6,6,64,128]{3,2,1,0:T(8,128)}, u32[]{:S(2)}) copy-start(f32[6,6,64,128]{3,2,1,0:T(8,128)} %param.14) | copy-start | bytes 3538948
  1.8 9.7 %collective-permute-start = (f32[1,6,64,128]{3,2,1,0:T(8,128)S(1)}, f32[1,6,64,128]{3,2,1,0:T(8,128)S(1)}, u32[]{:S(2)}, u32[]{:S(2)}) collective-permute-start(f32[1,6,64,128]{3,2,1,0:T(8,128)S(1)} %get-tuple-element.305), channel_id=1, source_target_pairs={{0,8},{8,16},{16,24},{24,0},{1,9},{9,17},{17,25},{25,1},{2,10},{10... | collective-permute-start | bytes 589832 | tf_op jit(solution)/shard_map/ppermute | solution.py:17
  4.8 10.3 %collective-permute-start.1 = (f32[1,6,64,128]{3,2,1,0:T(8,128)S(1)}, f32[1,6,64,128]{3,2,1,0:T(8,128)S(1)}, u32[]{:S(2)}, u32[]{:S(2)}) collective-permute-start(f32[1,6,64,128]{3,2,1,0:T(8,128)S(1)} %get-tuple-element.304), channel_id=1, source_target_pairs={{8,0},{16,8},{24,16},{0,24},{9,1},{17,9},{25,17},{1,25},{10,2},{18... | collective-permute-start | bytes 589832 | tf_op jit(solution)/shard_map/ppermute | solution.py:19
  11.6 8.6 %copy-start.26 = (s32[6,6,9]{2,1,0:T(8,128)S(1)}, s32[6,6,9]{2,1,0:T(8,128)}, u32[]{:S(2)}) copy-start(s32[6,6,9]{2,1,0:T(8,128)} %param.16) | copy-start | bytes 3892
  16.4 20.1 %collective-permute-start.2 = (f32[8,1,64,128]{3,2,1,0:T(8,128)S(1)}, f32[8,1,64,128]{3,2,1,0:T(8,128)S(1)}, u32[]{:S(2)}, u32[]{:S(2)}) collective-permute-start(f32[8,1,64,128]{3,2,1,0:T(8,128)S(1)} %get-tuple-element.296), channel_id=1, source_target_pairs={{0,1},{1,2},{2,3},{3,4},{4,5},{5,6},{6,7},{7,0},{8,9},{9,10},{10,1... | collective-permute-start | bytes 786440 | tf_op jit(solution)/shard_map/ppermute | solution.py:17
  16.4 20.0 %collective-permute-start.3 = (f32[8,1,64,128]{3,2,1,0:T(8,128)S(1)}, f32[8,1,64,128]{3,2,1,0:T(8,128)S(1)}, u32[]{:S(2)}, u32[]{:S(2)}) collective-permute-start(f32[8,1,64,128]{3,2,1,0:T(8,128)S(1)} %get-tuple-element.297), channel_id=1, source_target_pairs={{1,0},{2,1},{3,2},{4,3},{5,4},{6,5},{7,6},{0,7},{9,8},{10,9},{11,1... | collective-permute-start | bytes 786440 | tf_op jit(solution)/shard_map/ppermute | solution.py:19
  20.4 15.4 %copy-start.27 = (s32[6,6]{1,0:T(8,128)S(1)}, s32[6,6]{1,0:T(8,128)}, u32[]{:S(2)}) copy-start(s32[6,6]{1,0:T(8,128)} %param.18) | copy-start | bytes 436
  41.1 4.1 copy-start
  41.1 4.1 copy-start.2
  48.5 4.1 copy-start
  48.6 4.1 copy-start.2
  56.0 4.1 copy-start
  56.0 4.1 copy-start.2
  63.4 4.1 copy-start
  63.4 4.1 copy-start.2
  70.9 4.1 copy-start
  70.9 4.1 copy-start.2
  78.3 4.1 copy-start
  78.3 4.1 copy-start.2
  85.7 4.1 copy-start
  85.7 4.1 copy-start.2
  93.2 4.1 copy-start
  93.2 4.1 copy-start.2
  100.6 4.1 copy-start
  100.6 4.1 copy-start.2
  108.6 19.8 %copy-start.13 = (f32[36,64,128]{2,1,0:T(8,128)}, f32[36,64,128]{2,1,0:T(8,128)S(1)}, u32[]{:S(2)}) copy-start(f32[36,64,128]{2,1,0:T(8,128)S(1)} %constant_dynamic-update-slice_fusion.3) | copy-start | bytes 3538948
  108.7 8.0 %collective-permute-start.4 = (f32[1,6,64,128]{3,2,1,0:T(8,128)S(1)}, f32[1,6,64,128]{3,2,1,0:T(8,128)S(1)}, u32[]{:S(2)}, u32[]{:S(2)}) collective-permute-start(f32[1,6,64,128]{3,2,1,0:T(8,128)S(1)} %get-tuple-element.302), channel_id=1, source_target_pairs={{0,8},{8,16},{16,24},{24,0},{1,9},{9,17},{17,25},{25,1},{2,10},{10... | collective-permute-start | bytes 589832 | tf_op jit(solution)/shard_map/ppermute | solution.py:17
  110.2 7.4 %collective-permute-start.5 = (f32[1,6,64,128]{3,2,1,0:T(8,128)S(1)}, f32[1,6,64,128]{3,2,1,0:T(8,128)S(1)}, u32[]{:S(2)}, u32[]{:S(2)}) collective-permute-start(f32[1,6,64,128]{3,2,1,0:T(8,128)S(1)} %get-tuple-element.303), channel_id=1, source_target_pairs={{8,0},{16,8},{24,16},{0,24},{9,1},{17,9},{25,17},{1,25},{10,2},{18... | collective-permute-start | bytes 589832 | tf_op jit(solution)/shard_map/ppermute | solution.py:19
  118.4 9.4 %collective-permute-start.6 = (f32[8,1,64,128]{3,2,1,0:T(8,128)S(1)}, f32[8,1,64,128]{3,2,1,0:T(8,128)S(1)}, u32[]{:S(2)}, u32[]{:S(2)}) collective-permute-start(f32[8,1,64,128]{3,2,1,0:T(8,128)S(1)} %get-tuple-element.294), channel_id=1, source_target_pairs={{0,1},{1,2},{2,3},{3,4},{4,5},{5,6},{6,7},{7,0},{8,9},{9,10},{10,1... | collective-permute-start | bytes 786440 | tf_op jit(solution)/shard_map/ppermute | solution.py:17
  118.5 10.0 %collective-permute-start.7 = (f32[8,1,64,128]{3,2,1,0:T(8,128)S(1)}, f32[8,1,64,128]{3,2,1,0:T(8,128)}, u32[]{:S(2)}, u32[]{:S(2)}) collective-permute-start(f32[8,1,64,128]{3,2,1,0:T(8,128)S(1)} %get-tuple-element.295), channel_id=1, source_target_pairs={{1,0},{2,1},{3,2},{4,3},{5,4},{6,5},{7,6},{0,7},{9,8},{10,9},{11,1... | collective-permute-start | bytes 786440 | tf_op jit(solution)/shard_map/ppermute | solution.py:19
  132.9 4.1 copy-start.5
  132.9 4.1 copy-start.7
  140.4 4.1 copy-start.5
  140.4 4.1 copy-start.7
  147.9 4.1 copy-start.5
  147.9 4.1 copy-start.7
  155.3 4.1 copy-start.5
  155.3 4.1 copy-start.7
  162.8 4.1 copy-start.5
  162.8 4.1 copy-start.7
  170.3 4.1 copy-start.5
  170.3 4.1 copy-start.7
  177.7 4.1 copy-start.5
  177.7 4.1 copy-start.7
  185.2 4.1 copy-start.5
  185.2 4.1 copy-start.7
  192.7 4.1 copy-start.5
  201.3 19.5 %copy-start.15 = (f32[6,6,64,128]{3,2,1,0:T(8,128)}, f32[6,6,64,128]{3,2,1,0:T(8,128)S(1)}, u32[]{:S(2)}) copy-start(f32[6,6,64,128]{3,2,1,0:T(8,128)S(1)} %sub.47) | copy-start | bytes 3538948
  201.3 8.7 %collective-permute-start.8 = (f32[1,6,64,128]{3,2,1,0:T(8,128)S(1)}, f32[1,6,64,128]{3,2,1,0:T(8,128)S(1)}, u32[]{:S(2)}, u32[]{:S(2)}) collective-permute-start(f32[1,6,64,128]{3,2,1,0:T(8,128)S(1)} %get-tuple-element.300), channel_id=1, source_target_pairs={{0,8},{8,16},{16,24},{24,0},{1,9},{9,17},{17,25},{25,1},{2,10},{10... | collective-permute-start | bytes 589832 | tf_op jit(solution)/shard_map/ppermute | solution.py:17
  201.4 9.2 %collective-permute-start.9 = (f32[1,6,64,128]{3,2,1,0:T(8,128)S(1)}, f32[1,6,64,128]{3,2,1,0:T(8,128)S(1)}, u32[]{:S(2)}, u32[]{:S(2)}) collective-permute-start(f32[1,6,64,128]{3,2,1,0:T(8,128)S(1)} %get-tuple-element.301), channel_id=1, source_target_pairs={{8,0},{16,8},{24,16},{0,24},{9,1},{17,9},{25,17},{1,25},{10,2},{18... | collective-permute-start | bytes 589832 | tf_op jit(solution)/shard_map/ppermute | solution.py:19
  211.3 8.8 %collective-permute-start.10 = (f32[8,1,64,128]{3,2,1,0:T(8,128)S(1)}, f32[8,1,64,128]{3,2,1,0:T(8,128)S(1)}, u32[]{:S(2)}, u32[]{:S(2)}) collective-permute-start(f32[8,1,64,128]{3,2,1,0:T(8,128)S(1)} %get-tuple-element.292), channel_id=1, source_target_pairs={{0,1},{1,2},{2,3},{3,4},{4,5},{5,6},{6,7},{7,0},{8,9},{9,10},{10,1... | collective-permute-start | bytes 786440 | tf_op jit(solution)/shard_map/ppermute | solution.py:17
  211.4 9.4 %collective-permute-start.11 = (f32[8,1,64,128]{3,2,1,0:T(8,128)S(1)}, f32[8,1,64,128]{3,2,1,0:T(8,128)}, u32[]{:S(2)}, u32[]{:S(2)}) collective-permute-start(f32[8,1,64,128]{3,2,1,0:T(8,128)S(1)} %get-tuple-element.293), channel_id=1, source_target_pairs={{1,0},{2,1},{3,2},{4,3},{5,4},{6,5},{7,6},{0,7},{9,8},{10,9},{11,1... | collective-permute-start | bytes 786440 | tf_op jit(solution)/shard_map/ppermute | solution.py:19
  225.4 4.1 copy-start.9
  225.4 4.1 copy-start.11
  240.3 4.1 copy-start.9
  240.3 4.1 copy-start.11
  255.2 4.1 copy-start.9
  255.2 4.1 copy-start.11
  270.1 4.1 copy-start.9
  270.1 4.1 copy-start.11
  277.6 4.1 copy-start.9
  277.6 4.1 copy-start.11
  285.0 4.1 copy-start.9
  285.0 4.1 copy-start.11
  (72 other events, 86.0 us)
